TPU v7x, 32 devices: a whole 2x2x4 slice. The times are simulated.
32 devices in a mesh: seq: 8 (over z, y), head: 4 (over x, core).
Axes of the slice: x: 2, y: 2, z: 4, core: 2. Of those that a mesh axis runs over, the one named last changes fastest.
Arguments:
- tokens: bfloat16 [16384, 1024], P(('seq', 'head')), may hold values from -6 to 6
- mod_shift: float32 [1024], replicated, may hold values from -3 to 3
- mod_scale: float32 [1024], replicated, may hold values from -3 to 3
- attn_gate: float32 [1024], replicated, may hold values from -4 to 4
- w_qkv: bfloat16 [1024, 3072], replicated, may hold values from -0.1875 to 0.1875
- query_gain: float32 [1024], replicated, may hold values from 0.5 to 8
- key_gain: float32 [1024], replicated, may hold values from 0.5 to 8
- w_out: bfloat16 [1024, 1024], replicated, may hold values from -0.1875 to 0.1875
- w_dec: bfloat16 [1024, 128], replicated, may hold values from -0.1875 to 0.1875
- conv_weight: bfloat16 [3456, 128], replicated, may hold values from -0.109375 to 0.109375
- block_lists: int32 [256, 8], P('seq'), may hold values from 0 to 255, as said below
- active_blocks: int32 [32], replicated, may hold values from 4 to 8
- to_next: int32 [4096], P(('seq', 'head')), may hold values from 0 to 511
- to_prev: int32 [4096], P(('seq', 'head')), may hold values from 0 to 511
- conv_table: int32 [16384, 27], P(('seq', 'head')), may hold values from 0 to 768
Outputs:
- block_out: bfloat16 [16384, 1024], P(('seq', 'head'))
- decoded: bfloat16 [16384, 128], P(('seq', 'head'))
Inputs may be any that keep to these rules, and one draw needn't show every extreme that they name: `block_lists`: row g names block g first; all its entries lie within 16 blocks of the range of 32 blocks holding g: from max(0, (g // 32) * 32 - 16) to min(256, (g // 32 + 1) * 32 + 16) - 1, and both ends are named in every range that has them.
All inputs are finite; a program needn't handle non-finite values.
Results may differ from a plain program's by a relative error of at most 0.007.
The roundings to bfloat16 on the way count: a program that leaves them out, or rounds other values in their place, can miss the bound.
Values may be sent and summed in bfloat16 or wider, within the bound.
A program may use at most 128 MiB of HBM per device.

v0:
```python
import math

import jax
import jax.numpy as jnp
from jax import lax
from jax.sharding import PartitionSpec as P

D = 1024
HD = 64
BLK = 64
KB = 8
TAPS = 27
NB_DEV = 8


EPSILON = 1e-06
MASKED = -1000000000.0


def passed_along(value, axis, steps):
    count = lax.axis_size(axis)
    leading, last = (max(0, -steps), min(count, count - steps))
    return lax.ppermute(value, axis, [(source, source + steps) for source in range(leading, last)])


def layer_norm(values, mod_shift, mod_scale):
    centre = jnp.mean(values, axis=-1, keepdims=True)
    centred = values - centre
    spread = jnp.mean(centred * centred, axis=-1, keepdims=True)
    return centred * lax.rsqrt(spread + EPSILON) * (1.0 + mod_scale) + mod_shift


def head_norm(values, gain_row):
    per_head = values.reshape(values.shape[0], -1, HD)
    scaling = lax.rsqrt(jnp.mean(per_head * per_head, axis=-1, keepdims=True) + EPSILON)
    return (per_head * scaling).reshape(values.shape) * gain_row


def project(token_rows, mod_shift, mod_scale, w_qkv, query_gain, key_gain):
    normed = layer_norm(token_rows.astype(jnp.float32), mod_shift, mod_scale).astype(jnp.bfloat16)
    projected = jnp.dot(normed, w_qkv, preferred_element_type=jnp.float32)
    queries = head_norm(projected[:, :D], query_gain).astype(jnp.bfloat16)
    key_part = head_norm(projected[:, D : 2 * D], key_gain).astype(jnp.bfloat16)
    values = projected[:, 2 * D :].astype(jnp.bfloat16)
    return (queries, key_part, values)


def block_flags(block_ids, active_blocks):
    owners = block_ids // NB_DEV
    slot_index = block_ids % NB_DEV
    owner_ids = jnp.arange(active_blocks.shape[0], dtype=jnp.int32)
    counted = jnp.sum(jnp.where(owners[..., None] == owner_ids, active_blocks, 0), axis=-1)
    return slot_index < counted


def attend(queries, key_rows, value_rows, live_keys):
    scores = jnp.einsum(
        "bqhd,bkhd->bhqk", queries, key_rows, preferred_element_type=jnp.float32
    ) * (1.0 / math.sqrt(HD))
    penalty = jnp.where(jnp.repeat(live_keys, BLK, axis=1), jnp.float32(0.0), jnp.float32(MASKED))
    scores = scores + penalty[:, None, None, :]
    highest = jnp.max(scores, axis=-1, keepdims=True)
    raised = jnp.exp(scores - highest)
    weights = (raised / jnp.sum(raised, axis=-1, keepdims=True)).astype(jnp.bfloat16)
    output = jnp.einsum("bhqk,bkhd->bqhd", weights, value_rows, preferred_element_type=jnp.float32)
    return output.astype(jnp.bfloat16)


def body(
    tokens,
    mod_shift,
    mod_scale,
    attn_gate,
    w_qkv,
    query_gain,
    key_gain,
    w_out,
    w_dec,
    conv_weight,
    block_lists,
    active_blocks,
    to_next,
    to_prev,
    conv_table,
):
    slot_count = tokens.shape[0]
    head_count = lax.axis_size("head")
    seq_index = lax.axis_index("seq")
    device = seq_index * head_count + lax.axis_index("head")
    owner_ids = jnp.arange(active_blocks.shape[0], dtype=jnp.int32)
    own_active = jnp.sum(jnp.where(owner_ids == device, active_blocks, 0))
    live_rows = jnp.arange(slot_count, dtype=jnp.int32) < own_active * BLK
    queries, key_part, values = project(tokens, mod_shift, mod_scale, w_qkv, query_gain, key_gain)
    query_group, key_group, value_group = (
        lax.all_to_all(queries, "head", split_axis=1, concat_axis=0, tiled=True),
        lax.all_to_all(key_part, "head", split_axis=1, concat_axis=0, tiled=True),
        lax.all_to_all(values, "head", split_axis=1, concat_axis=0, tiled=True),
    )
    group_rows = query_group.shape[0]
    local_width = query_group.shape[1]
    group_blocks = group_rows // BLK
    heads_here = local_width // HD
    key_value = jnp.concatenate([key_group, value_group], axis=1)
    before = passed_along(key_value, "seq", 1)
    behind = passed_along(key_value, "seq", -1)
    reachable = jnp.concatenate([before, key_value, behind], axis=0)
    first_block = (seq_index - 1) * group_blocks
    reach_blocks = reachable.reshape(-1, BLK, 2 * local_width)
    local_ids = block_lists - first_block
    live_lists = block_flags(block_lists, active_blocks)
    per_step = math.gcd(group_blocks, max(1, 512 // BLK))
    step_count = group_blocks // per_step
    query_blocks = query_group.reshape(step_count, per_step, BLK, heads_here, HD)

    def one_step(inputs):
        query_part, picked_ids, live_keys = inputs
        picked = reach_blocks[picked_ids.reshape(-1)]
        key_rows = picked[:, :, :local_width].reshape(per_step, KB * BLK, heads_here, HD)
        value_rows = picked[:, :, local_width:].reshape(per_step, KB * BLK, heads_here, HD)
        return attend(query_part, key_rows, value_rows, live_keys)

    attended = lax.map(
        one_step,
        (
            query_blocks,
            local_ids.reshape(step_count, per_step, KB),
            live_lists.reshape(step_count, per_step, KB),
        ),
    )
    attended = attended.reshape(group_rows, local_width)
    returned = lax.all_to_all(attended, "head", split_axis=0, concat_axis=1, tiled=True)
    update = jnp.dot(returned, w_out, preferred_element_type=jnp.float32)
    residual = tokens.astype(jnp.float32) + attn_gate * update
    block_out = jnp.where(live_rows[:, None], residual, jnp.float32(0.0)).astype(jnp.bfloat16)
    features = jnp.dot(block_out, w_dec, preferred_element_type=jnp.float32).astype(jnp.bfloat16)
    sent_next = features[to_next]
    sent_prev = features[to_prev]
    from_prev = passed_along(sent_next, ("seq", "head"), 1)
    from_next = passed_along(sent_prev, ("seq", "head"), -1)
    channels = features.shape[1]
    buffer = jnp.concatenate(
        [features, from_prev, from_next, jnp.zeros((1, channels), jnp.bfloat16)], axis=0
    )
    tap_rows = buffer[conv_table.reshape(-1)].reshape(slot_count, TAPS * channels)
    conv_out = jnp.dot(tap_rows, conv_weight, preferred_element_type=jnp.float32)
    decoded = jnp.where(
        live_rows[:, None], features.astype(jnp.float32) + conv_out, jnp.float32(0.0)
    ).astype(jnp.bfloat16)
    return (block_out, decoded)


def solution(mesh):
    return jax.shard_map(
        body,
        mesh=mesh,
        in_specs=(
            P(("seq", "head"), None),
            P(),
            P(),
            P(),
            P(),
            P(),
            P(),
            P(),
            P(),
            P(),
            P("seq", None),
            P(),
            P(("seq", "head")),
            P(("seq", "head")),
            P(("seq", "head"), None),
        ),
        out_specs=(P(("seq", "head"), None), P(("seq", "head"), None)),
        check_vma=False,
    )
```

profile of v0, /device:TPU:3, one launch (start us, length us, event | category | flops | bytes accessed | tf_op | source)
XLA Modules:
  0.0 434.4 jit_solution(10074167695321712992)
XLA Ops:
  45.4 9.8 %all-to-all-done = bf16[512,4,256]{2,0,1:T(8,128)(2,1)S(1)} async-done(((bf16[512,4,256]{2,0,1:T(8,128)(2,1)}), bf16[512,4,256]{2,0,1:T(8,128)(2,1)S(1)}, u32[]{:S(2)}, u32[]{:S(2)}) %all-to-all-start) | async-done | bytes 1048608 | tf_op jit(solution)/shard_map/all_to_all | solution.py:96
  55.2 17.9 %all_to_all.73 = bf16[512,4,256]{2,0,1:T(8,128)(2,1)S(1)} all-to-all(bf16[512,4,256]{2,0,1:T(8,128)(2,1)} %bitcast.72), channel_id=1, replica_groups=mesh['seq'=8,'head'=4] {'head'}, dimensions={1} | all-to-all | bytes 2097152 | tf_op jit(solution)/shard_map/all_to_all | solution.py:97
  83.6 6.4 %all-to-all-start.2 = ((bf16[512,4,256]{0,2,1:T(8,128)(2,1)}), bf16[512,4,256]{0,2,1:T(8,128)(2,1)}, u32[]{:S(2)}, u32[]{:S(2)}) async-start(bf16[512,4,256]{0,2,1:T(8,128)(2,1)} %bitcast.70), calls=%async_computation.2 | async-start | bytes 2097152 | tf_op jit(solution)/shard_map/all_to_all | solution.py:95
  93.6 9.0 %all-to-all-done.2 = bf16[512,4,256]{0,2,1:T(8,128)(2,1)} async-done(((bf16[512,4,256]{0,2,1:T(8,128)(2,1)}), bf16[512,4,256]{0,2,1:T(8,128)(2,1)}, u32[]{:S(2)}, u32[]{:S(2)}) %all-to-all-start.2) | async-done | bytes 1048608 | tf_op jit(solution)/shard_map/all_to_all | solution.py:95
  106.5 61.8 %collective-permute-done = bf16[2048,512]{1,0:T(8,128)(2,1)} collective-permute-done((bf16[2048,512]{1,0:T(8,128)(2,1)}, bf16[2048,512]{1,0:T(8,128)(2,1)}, u32[]{:S(2)}, u32[]{:S(2)}) %collective-permute-start) | collective-permute-done | bytes 2097184 | tf_op jit(solution)/shard_map/ppermute | solution.py:23
  168.2 6.0 %pad_maximum_fusion = bf16[6144,512]{1,0:T(8,128)(2,1)} fusion(bf16[2048,512]{1,0:T(8,128)(2,1)} %collective-permute-done.1, bf16[2048,256]{1,0:T(8,128)(2,1)} %bitcast.66, bf16[2048,256]{1,0:T(8,128)(2,1)S(1)} %bitcast.64, bf16[2048,512]{1,0:T(8,128)(2,1)} %collective-permute-done), kind=kLoop, calls=%fused_computation.27 | loop fusion | flops 25165824 | bytes 12582912 | tf_op jit(solution)/shard_map/concatenate | solution.py:106
  174.3 179.5 %while.10 = (s32[]{:T(128)}, bf16[4,8,64,4,64]{2,1,4,3,0:T(8,128)(2,1)}, s32[4,8,8]{2,1,0:T(8,128)S(1)}, bf16[96,64,512]{2,1,0:T(8,128)(2,1)}, bf16[4,8,64,4,64]...) while((s32[]{:T(128)}, bf16[4,8,64,4,64]{2,1,4,3,0:T(8,128)(2,1)}, ...), condition=%wide.region_9.10_spmd, body=%wide.region_6.9_spmd.sunk | while | flops 276956928 | bytes 48585880 | solution.py:122
  184.8 7.0 %reshape.215 = bf16[8,512,4,64]{3,2,1,0:T(4,128)(2,1)} reshape(bf16[64,64,256]{2,1,0:T(8,128)(2,1)} %get-tuple-element.108) | data formatting | bytes 4194304 | tf_op jit(solution)/shard_map/while/body/eval_jaxpr/reshape | solution.py:118
  199.3 6.6 %fusion.63 = (f32[8,4,64]{2,1,0:T(4,128)S(1)}, f32[8,4,64,512]{3,2,1,0:T(8,128)}) fusion(f32[8,4,64,512]{3,2,1,0:T(8,128)} %fusion.62, f32[8,512]{1,0:T(8,128)S(1)} %select_n.108), kind=kOutput, calls=%fused_computation.88.clone.1 | output fusion | flops 6291967 | bytes 8413184 | tf_op jit(solution)/shard_map/while/body/eval_jaxpr/sub | solution.py:63
  205.9 7.0 %reshape.216 = bf16[8,512,4,64]{3,2,1,0:T(4,128)(2,1)} reshape(bf16[64,64,256]{2,1,0:T(8,128)(2,1)} %get-tuple-element.111) | data formatting | bytes 4194304 | tf_op jit(solution)/shard_map/while/body/eval_jaxpr/reshape | solution.py:119
  229.6 7.0 %reshape.215 = bf16[8,512,4,64]{3,2,1,0:T(4,128)(2,1)} reshape(bf16[64,64,256]{2,1,0:T(8,128)(2,1)} %get-tuple-element.108) | data formatting | bytes 4194304 | tf_op jit(solution)/shard_map/while/body/eval_jaxpr/reshape | solution.py:118
  244.2 6.6 %fusion.63 = (f32[8,4,64]{2,1,0:T(4,128)S(1)}, f32[8,4,64,512]{3,2,1,0:T(8,128)}) fusion(f32[8,4,64,512]{3,2,1,0:T(8,128)} %fusion.62, f32[8,512]{1,0:T(8,128)S(1)} %select_n.108), kind=kOutput, calls=%fused_computation.88.clone.1 | output fusion | flops 6291967 | bytes 8413184 | tf_op jit(solution)/shard_map/while/body/eval_jaxpr/sub | solution.py:63
  250.8 7.0 %reshape.216 = bf16[8,512,4,64]{3,2,1,0:T(4,128)(2,1)} reshape(bf16[64,64,256]{2,1,0:T(8,128)(2,1)} %get-tuple-element.111) | data formatting | bytes 4194304 | tf_op jit(solution)/shard_map/while/body/eval_jaxpr/reshape | solution.py:119
  274.5 7.0 %reshape.215 = bf16[8,512,4,64]{3,2,1,0:T(4,128)(2,1)} reshape(bf16[64,64,256]{2,1,0:T(8,128)(2,1)} %get-tuple-element.108) | data formatting | bytes 4194304 | tf_op jit(solution)/shard_map/while/body/eval_jaxpr/reshape | solution.py:118
  289.0 6.6 %fusion.63 = (f32[8,4,64]{2,1,0:T(4,128)S(1)}, f32[8,4,64,512]{3,2,1,0:T(8,128)}) fusion(f32[8,4,64,512]{3,2,1,0:T(8,128)} %fusion.62, f32[8,512]{1,0:T(8,128)S(1)} %select_n.108), kind=kOutput, calls=%fused_computation.88.clone.1 | output fusion | flops 6291967 | bytes 8413184 | tf_op jit(solution)/shard_map/while/body/eval_jaxpr/sub | solution.py:63
  295.7 7.0 %reshape.216 = bf16[8,512,4,64]{3,2,1,0:T(4,128)(2,1)} reshape(bf16[64,64,256]{2,1,0:T(8,128)(2,1)} %get-tuple-element.111) | data formatting | bytes 4194304 | tf_op jit(solution)/shard_map/while/body/eval_jaxpr/reshape | solution.py:119
  319.4 7.0 %reshape.215 = bf16[8,512,4,64]{3,2,1,0:T(4,128)(2,1)} reshape(bf16[64,64,256]{2,1,0:T(8,128)(2,1)} %get-tuple-element.108) | data formatting | bytes 4194304 | tf_op jit(solution)/shard_map/while/body/eval_jaxpr/reshape | solution.py:118
  333.9 6.6 %fusion.63 = (f32[8,4,64]{2,1,0:T(4,128)S(1)}, f32[8,4,64,512]{3,2,1,0:T(8,128)}) fusion(f32[8,4,64,512]{3,2,1,0:T(8,128)} %fusion.62, f32[8,512]{1,0:T(8,128)S(1)} %select_n.108), kind=kOutput, calls=%fused_computation.88.clone.1 | output fusion | flops 6291967 | bytes 8413184 | tf_op jit(solution)/shard_map/while/body/eval_jaxpr/sub | solution.py:63
  340.6 7.0 %reshape.216 = bf16[8,512,4,64]{3,2,1,0:T(4,128)(2,1)} reshape(bf16[64,64,256]{2,1,0:T(8,128)(2,1)} %get-tuple-element.111) | data formatting | bytes 4194304 | tf_op jit(solution)/shard_map/while/body/eval_jaxpr/reshape | solution.py:119
  357.9 6.6 %all-to-all-start.3 = ((bf16[4,512,256]{1,2,0:T(8,128)(2,1)}), bf16[4,512,256]{1,2,0:T(8,128)(2,1)}, u32[]{:S(2)}, u32[]{:S(2)}) async-start(bf16[4,512,256]{1,2,0:T(8,128)(2,1)} %all_to_all.65), calls=%async_computation.3 | async-start | bytes 2097152 | tf_op jit(solution)/shard_map/all_to_all | solution.py:131
  364.7 12.3 %all-to-all-done.3 = bf16[4,512,256]{1,2,0:T(8,128)(2,1)} async-done(((bf16[4,512,256]{1,2,0:T(8,128)(2,1)}), bf16[4,512,256]{1,2,0:T(8,128)(2,1)}, u32[]{:S(2)}, u32[]{:S(2)}) %all-to-all-start.3) | async-done | bytes 1048608 | tf_op jit(solution)/shard_map/all_to_all | solution.py:131
  381.8 5.8 %collective-permute-start.2 = (bf16[128,128]{1,0:T(8,128)(2,1)S(1)}, bf16[128,128]{1,0:T(8,128)(2,1)S(1)}, u32[]{:S(2)}, u32[]{:S(2)}) collective-permute-start(bf16[128,128]{1,0:T(8,128)(2,1)S(1)} %gather_fusion.1), channel_id=1, source_target_pairs={{0,1},{1,2},{2,3},{3,4},{4,5},{5,6},{6,7},{7,8},{8,9},{9,10},{10,1... | collective-permute-start | bytes 98312 | tf_op jit(solution)/shard_map/ppermute | solution.py:23
  394.6 28.4 %gather_fusion.3 = bf16[13824,128]{1,0:T(8,128)(2,1)} fusion(bf16[769,128]{1,0:T(8,128)(2,1)S(1)} %maximum_maximum_fusion, s32[14336]{0:T(1024)S(1)} %pad_clamp_fusion.1), kind=kCustom, calls=%fused_computation.3 | custom fusion | bytes 7133184 | tf_op jit(solution)/shard_map/gather | solution.py:144
  423.0 7.6 %reshape.168 = bf16[512,3456]{1,0:T(8,128)(2,1)} reshape(bf16[13824,128]{1,0:T(8,128)(2,1)} %gather_fusion.3) | data formatting | bytes 7077888 | tf_op jit(solution)/shard_map/reshape | solution.py:144
  (146 shorter events, 178.1 us)
Async XLA Ops:
  0.6 376.4 %copy-start = (bf16[1024,1024]{1,0:T(8,128)(2,1)S(1)}, bf16[1024,1024]{1,0:T(8,128)(2,1)}, u32[]{:S(2)}) copy-start(bf16[1024,1024]{1,0:T(8,128)(2,1)} %param.24) | copy-start | bytes 6291460
  0.6 3.3 copy-start.3
  0.7 3.3 copy-start.10
  0.7 3.3 copy-start.13
  9.7 4.0 copy-start.1
  29.4 3.0 copy-start.8
  29.4 3.0 copy-start.9
  39.0 16.2 %all-to-all-start = ((bf16[512,4,256]{2,0,1:T(8,128)(2,1)}), bf16[512,4,256]{2,0,1:T(8,128)(2,1)S(1)}, u32[]{:S(2)}, u32[]{:S(2)}) async-start(bf16[512,4,256]{2,0,1:T(8,128)(2,1)} %bitcast.71), calls=%async_computation | async-start | bytes 2097152 | tf_op jit(solution)/shard_map/all_to_all | solution.py:96
  73.1 1.7 copy-start.2
  74.8 93.5 %collective-permute-start = (bf16[2048,512]{1,0:T(8,128)(2,1)}, bf16[2048,512]{1,0:T(8,128)(2,1)}, u32[]{:S(2)}, u32[]{:S(2)}) collective-permute-start(bf16[2048,512]{1,0:T(8,128)(2,1)} %pad_maximum_fusion.1), channel_id=1, source_target_pairs={{0,4},{4,8},{8,12},{12,16},{16,20},{20,24},{24,28},{1,5},{5,9},{9,... | collective-permute-start | bytes 6291464 | tf_op jit(solution)/shard_map/ppermute | solution.py:23
  80.0 88.2 %collective-permute-start.1 = (bf16[2048,512]{1,0:T(8,128)(2,1)}, bf16[2048,512]{1,0:T(8,128)(2,1)}, u32[]{:S(2)}, u32[]{:S(2)}) collective-permute-start(bf16[2048,512]{1,0:T(8,128)(2,1)} %pad_maximum_fusion.1), channel_id=1, source_target_pairs={{4,0},{8,4},{12,8},{16,12},{20,16},{24,20},{28,24},{5,1},{9,5},{13... | collective-permute-start | bytes 6291464 | tf_op jit(solution)/shard_map/ppermute | solution.py:23
  81.3 8.7 %copy-start.7 = (s32[32,8]{0,1:T(8,128)S(1)}, s32[32,8]{0,1:T(8,128)}, u32[]{:S(2)}) copy-start(s32[32,8]{0,1:T(8,128)} %param.27) | copy-start | bytes 3076
  81.3 10.1 %copy-start.11 = (s32[32]{0:T(128)S(1)}, s32[32]{0:T(128)}, u32[]{:S(2)}) copy-start(s32[32]{0:T(128)} %param.28) | copy-start | bytes 388
  83.6 19.0 %all-to-all-start.2 = ((bf16[512,4,256]{0,2,1:T(8,128)(2,1)}), bf16[512,4,256]{0,2,1:T(8,128)(2,1)}, u32[]{:S(2)}, u32[]{:S(2)}) async-start(bf16[512,4,256]{0,2,1:T(8,128)(2,1)} %bitcast.70), calls=%async_computation.2 | async-start | bytes 2097152 | tf_op jit(solution)/shard_map/all_to_all | solution.py:95
  353.8 10.7 %copy-start.15 = (s32[128]{0:T(128)S(1)}, s32[128]{0:T(128)}, u32[]{:S(2)}) copy-start(s32[128]{0:T(128)} %param.29) | copy-start | bytes 1540
  353.8 10.7 %copy-start.16 = (s32[128]{0:T(128)S(1)}, s32[128]{0:T(128)}, u32[]{:S(2)}) copy-start(s32[128]{0:T(128)} %param.30) | copy-start | bytes 1540
  353.8 23.2 %copy-start.4 = (bf16[512,1024]{1,0:T(8,128)(2,1)S(1)}, bf16[512,1024]{1,0:T(8,128)(2,1)}, u32[]{:S(2)}) copy-start(bf16[512,1024]{1,0:T(8,128)(2,1)} %param.17) | copy-start | bytes 3145732
  353.8 23.2 %copy-start.14 = (f32[1024]{0:T(1024)S(1)}, f32[1024]{0:T(1024)}, u32[]{:S(2)}) copy-start(f32[1024]{0:T(1024)} %param.20) | copy-start | bytes 12292
  357.9 19.1 %all-to-all-start.3 = ((bf16[4,512,256]{1,2,0:T(8,128)(2,1)}), bf16[4,512,256]{1,2,0:T(8,128)(2,1)}, u32[]{:S(2)}, u32[]{:S(2)}) async-start(bf16[4,512,256]{1,2,0:T(8,128)(2,1)} %all_to_all.65), calls=%async_computation.3 | async-start | bytes 2097152 | tf_op jit(solution)/shard_map/all_to_all | solution.py:131
  377.0 3.6 copy-start.6
  379.6 1.0 copy-start.5
  381.8 8.5 %collective-permute-start.2 = (bf16[128,128]{1,0:T(8,128)(2,1)S(1)}, bf16[128,128]{1,0:T(8,128)(2,1)S(1)}, u32[]{:S(2)}, u32[]{:S(2)}) collective-permute-start(bf16[128,128]{1,0:T(8,128)(2,1)S(1)} %gather_fusion.1), channel_id=1, source_target_pairs={{0,1},{1,2},{2,3},{3,4},{4,5},{5,6},{6,7},{7,8},{8,9},{9,10},{10,1... | collective-permute-start | bytes 98312 | tf_op jit(solution)/shard_map/ppermute | solution.py:23
  388.3 6.1 %collective-permute-start.3 = (bf16[128,128]{1,0:T(8,128)(2,1)S(1)}, bf16[128,128]{1,0:T(8,128)(2,1)S(1)}, u32[]{:S(2)}, u32[]{:S(2)}) collective-permute-start(bf16[128,128]{1,0:T(8,128)(2,1)S(1)} %gather_fusion.2), channel_id=1, source_target_pairs={{1,0},{2,1},{3,2},{4,3},{5,4},{6,5},{7,6},{8,7},{9,8},{10,9},{11,1... | collective-permute-start | bytes 98312 | tf_op jit(solution)/shard_map/ppermute | solution.py:23
  423.0 7.6 %copy-start.12 = (bf16[3456,128]{1,0:T(8,128)(2,1)S(1)}, bf16[3456,128]{1,0:T(8,128)(2,1)}, u32[]{:S(2)}) copy-start(bf16[3456,128]{1,0:T(8,128)(2,1)} %param.26) | copy-start | bytes 2654212
where the time goes:
time: 439 us; the launch traced here: 434 us
  local copies, waits for them, and re-layouts  180 us (41%)
  waiting for transfers between devices  97 us (22%)
  matrix products  55.9 us (13%)
  other arithmetic  51.4 us (12%)
  starting transfers between devices  30.8 us (7%)
  blocking collectives  17.9 us (4%)
    ppermute x4, waiting for transfers between devices, passed_along(): lax.ppermute(value, axis, [(source, source + steps) for source in range(l...  66 us
    gather x1, local copies, waits for them, and re-layouts, body(): buffer[conv_table.reshape(-1)].reshape(slot_count, TAPS * channels)  28.4 us
    reshape x4, local copies, waits for them, and re-layouts, one_step(): picked[:, :, local_width:].reshape(per_step, KB * BLK, heads_here, HD)  28.2 us
    reshape x4, local copies, waits for them, and re-layouts, one_step(): picked[:, :, :local_width].reshape(per_step, KB * BLK, heads_here, HD)  28.1 us
    sub x4, other arithmetic, attend(): raised = jnp.exp(scores - highest)  26.5 us
    dot_general x4, matrix products, attend(): jnp.einsum('bqhd,bkhd->bhqk', queries, key_rows, preferred_element_type=j...  23.3 us
    gather x4, local copies, waits for them, and re-layouts, one_step(): picked = reach_blocks[picked_ids.reshape(-1)]  22.5 us
    dot_general x4, matrix products, attend(): jnp.einsum('bhqk,bkhd->bqhd', weights, value_rows, preferred_element_type...  20.1 us
  transfers between devices with their start and end apart: 7, of which 5 were waited for; matrix products, arithmetic and copies ran while one was open for 3% of the time, Pallas kernels for 0%

commit v1 on v0

v1 whole, which is shorter than its diff:
```python
import functools
import math

import jax
import jax.numpy as jnp
from jax import lax
from jax.experimental import pallas as pl
from jax.experimental.pallas import tpu as pltpu
from jax.sharding import PartitionSpec as P

HD = 64
BLK = 64
NB = 8
KB = 8
EPSILON = 1e-06
MASKED = -1000000000.0
MESH = pl.DeviceIdType.MESH
BF16 = jnp.bfloat16
F32 = jnp.float32


def project_kernel(
    S, H,
    tokens, mod_shift, mod_scale, w_qkv, q_gain, k_gain,
    q, kv,
    normed, kv_send, q_send, own_sem,
    kv_ssem, kv_rsem, f_ssem, q_ssem, q_rsem,
):
    T, D = tokens.shape
    W = D // H
    half = H // 2
    s = lax.axis_index("seq")
    h = lax.axis_index("head")

    def peer_of(i):
        return ((h // 2 + i // 2) % half) * 2 + (h % 2 + i % 2) % 2

    has_next, has_prev = s < S - 1, s > 0

    barrier = pltpu.get_barrier_semaphore()
    for i in range(1, H):
        pl.semaphore_signal(barrier, inc=1, device_id=(s, peer_of(i)), device_id_type=MESH)
    for cond, where in ((has_next, (s + 1, h)), (has_prev, (s - 1, h))):
        @pl.when(cond)
        def _():
            pl.semaphore_signal(barrier, inc=1, device_id=where, device_id_type=MESH)

    RT = 64

    def norm_rows(r, _):
        rows = pl.ds(pl.multiple_of(r * RT, RT), RT)
        x = tokens[rows, :].astype(F32)
        centred = x - jnp.mean(x, axis=-1, keepdims=True)
        spread = jnp.mean(centred * centred, axis=-1, keepdims=True)
        y = centred * lax.rsqrt(spread + EPSILON) * (1.0 + mod_scale[...]) + mod_shift[...]
        normed[rows, :] = y.astype(BF16)
        return 0

    lax.fori_loop(0, T // RT, norm_rows, 0)

    pl.semaphore_wait(
        barrier, H - 1 + jnp.where(has_next, jnp.int32(1), jnp.int32(0)) + jnp.where(has_prev, jnp.int32(1), jnp.int32(0))
    )

    same = (
        lax.broadcasted_iota(jnp.int32, (W, W), 0) // HD
        == lax.broadcasted_iota(jnp.int32, (W, W), 1) // HD
    )
    averaging = jnp.where(same, F32(1.0 / HD), F32(0.0)).astype(BF16)

    def head_norm(x, gain):
        square = x * x
        high = square.astype(BF16)
        low = (square - high.astype(F32)).astype(BF16)
        mean = jnp.dot(high, averaging, preferred_element_type=F32) + jnp.dot(
            low, averaging, preferred_element_type=F32
        )
        return (x * lax.rsqrt(mean + EPSILON) * gain).astype(BF16)

    PT = min(256, T)

    def columns(part, owner):
        return pl.ds(pl.multiple_of(part * D + owner * W, W), W)

    def gains(ref, owner):
        return ref[:, pl.ds(pl.multiple_of(owner * W, W), W)]

    def make_kv(dst, slot, owner):
        def step(r, _):
            rows = pl.ds(pl.multiple_of(r * PT, PT), PT)
            x = normed[rows, :]
            key = jnp.dot(x, w_qkv[:, columns(1, owner)], preferred_element_type=F32)
            dst[slot, rows, 0:W] = head_norm(key, gains(k_gain, owner))
            val = jnp.dot(x, w_qkv[:, columns(2, owner)], preferred_element_type=F32)
            dst[slot, rows, W : 2 * W] = val.astype(BF16)
            return 0

        lax.fori_loop(0, T // PT, step, 0)

    def make_q(dst, slot, owner):
        def step(r, _):
            rows = pl.ds(pl.multiple_of(r * PT, PT), PT)
            x = jnp.dot(normed[rows, :], w_qkv[:, columns(0, owner)], preferred_element_type=F32)
            dst[slot, rows, :] = head_norm(x, gains(q_gain, owner))
            return 0

        lax.fori_loop(0, T // PT, step, 0)

    def kv_copy(i):
        return pltpu.make_async_remote_copy(
            src_ref=kv_send.at[i],
            dst_ref=kv.at[half + h],
            send_sem=kv_ssem.at[i],
            recv_sem=kv_rsem.at[half + h],
            device_id=(s, peer_of(i)),
            device_id_type=MESH,
        )

    def q_copy(i):
        return pltpu.make_async_remote_copy(
            src_ref=q_send.at[i],
            dst_ref=q.at[h],
            send_sem=q_ssem.at[i],
            recv_sem=q_rsem.at[h],
            device_id=(s, peer_of(i)),
            device_id_type=MESH,
        )

    def forward_copy(i, slot, target):
        return pltpu.make_async_remote_copy(
            src_ref=kv_send.at[0] if i == 0 else kv.at[half + peer_of(i)],
            dst_ref=kv.at[slot],
            send_sem=f_ssem.at[i],
            recv_sem=kv_rsem.at[slot],
            device_id=(target, h),
            device_id_type=MESH,
        )

    def each_forward(i, act):
        owner = peer_of(i)

        @pl.when(jnp.logical_and(owner >= half, has_next))
        def _():
            act(forward_copy(i, owner - half, s + 1))

        @pl.when(jnp.logical_and(owner < half, has_prev))
        def _():
            act(forward_copy(i, half + H + owner, s - 1))

    def kv_arrival(slot):
        pltpu.make_async_copy(kv.at[slot], kv.at[slot], kv_rsem.at[slot]).wait()

    own_kv = pltpu.make_async_copy(kv_send.at[0], kv.at[half + h], own_sem.at[0])
    own_q = pltpu.make_async_copy(q_send.at[0], q.at[h], own_sem.at[1])
    order = list(range(2, H)) + [1]
    make_kv(kv_send, 0, h)
    each_forward(0, lambda c: c.start())
    own_kv.start()
    for i in order:
        make_kv(kv_send, i, peer_of(i))
        kv_copy(i).start()
    kv_arrival(half + peer_of(1))
    each_forward(1, lambda c: c.start())
    for i in order:
        make_q(q_send, i, peer_of(i))
        q_copy(i).start()
    make_q(q_send, 0, h)
    own_q.start()
    for i in range(2, H):
        kv_arrival(half + peer_of(i))
        each_forward(i, lambda c: c.start())
    for i in range(1, H):
        pltpu.make_async_copy(q.at[peer_of(i)], q.at[peer_of(i)], q_rsem.at[peer_of(i)]).wait()
    for j in range(half):
        @pl.when(has_prev)
        def _():
            kv_arrival(j)

        @pl.when(has_next)
        def _():
            kv_arrival(half + H + j)

    own_kv.wait()
    own_q.wait()
    for i in range(1, H):
        kv_copy(i).wait_send()
        q_copy(i).wait_send()
    for i in range(H):
        each_forward(i, lambda c: c.wait_send())


def attend_kernel(lists, active, q, kv, o):
    H, T, W = q.shape
    heads = W // HD
    group = lax.axis_index("seq") * H
    o[...] = jnp.zeros_like(o)
    rows_of = lax.broadcasted_iota(jnp.int32, (heads * BLK, W), 0) // BLK
    lanes_of = lax.broadcasted_iota(jnp.int32, (heads * BLK, W), 1) // HD
    diagonal = jnp.where(rows_of == lanes_of, F32(1.0 / math.sqrt(HD)), F32(0.0)).astype(BF16)
    block_of = lax.broadcasted_iota(jnp.int32, (1, KB * BLK), 1) // BLK
    lane_head = lax.broadcasted_iota(jnp.int32, (BLK, W), 1) // HD
    base = (lax.axis_index("seq") * H - H // 2) * NB

    def attend(owner, b):
        rows = pl.ds(pl.multiple_of(b * BLK, BLK), BLK)
        query = q[owner, rows, :]
        spread = jnp.concatenate([query] * heads, axis=0) * diagonal
        keys, values = [], []
        penalty = jnp.zeros((1, KB * BLK), F32)
        for n in range(KB):
            block = lists[owner * NB + b, n]
            live = lax.rem(block, NB) < active[block // NB]
            penalty = jnp.where(
                block_of == n, jnp.where(live, F32(0.0), F32(MASKED)), penalty
            )
            local = block - base
            keys.append(kv[local, :, 0:W])
            values.append(kv[local, :, W : 2 * W])
        scores = lax.dot_general(
            spread, jnp.concatenate(keys, axis=0), (((1,), (1,)), ((), ())),
            preferred_element_type=F32,
        ) + penalty
        raised = jnp.exp(scores - jnp.max(scores, axis=-1, keepdims=True))
        weights = (raised * (1.0 / jnp.sum(raised, axis=-1, keepdims=True))).astype(BF16)
        mixed = jnp.dot(weights, jnp.concatenate(values, axis=0), preferred_element_type=F32)
        result = mixed[0:BLK, :]
        for n in range(1, heads):
            result = jnp.where(lane_head == n, mixed[n * BLK : (n + 1) * BLK, :], result)
        o[owner, rows, :] = result.astype(BF16)

    def each_owner(owner, _):
        def pair(b, _):
            attend(owner, 2 * b)
            attend(owner, 2 * b + 1)
            return 0

        return lax.fori_loop(0, (active[group + owner] + 1) // 2, pair, 0)

    lax.fori_loop(0, H, each_owner, 0)


def finish_kernel(
    S, H,
    tokens, attn_gate, o, w_out, w_dec, conv_w, active, to_next, to_prev, table,
    block_out, decoded,
    att, acc, onehot, buf, face, own_sem, o_ssem, o_rsem, face_ssem, face_rsem,
):
    T, D = tokens.shape
    W = D // H
    C = w_dec.shape[1]
    TAPS = table.shape[1]
    FACE = to_next.shape[0]
    half = H // 2
    RT = 64
    s = lax.axis_index("seq")
    h = lax.axis_index("head")

    def peer_of(i):
        return ((h // 2 + i // 2) % half) * 2 + (h % 2 + i % 2) % 2

    has_next, has_prev = s < S - 1, s > 0
    wrap_next = jnp.logical_and(h == H - 1, has_next)
    wrap_prev = jnp.logical_and(h == 0, has_prev)

    barrier = pltpu.get_barrier_semaphore()
    for i in range(1, H):
        pl.semaphore_signal(barrier, inc=1, device_id=(s, peer_of(i)), device_id_type=MESH)
    for cond, where in ((wrap_next, (s + 1, 0)), (wrap_prev, (s - 1, H - 1))):
        @pl.when(cond)
        def _():
            pl.semaphore_signal(barrier, inc=1, device_id=where, device_id_type=MESH)
    pl.semaphore_wait(
        barrier, H - 1 + jnp.where(wrap_next, jnp.int32(1), jnp.int32(0)) + jnp.where(wrap_prev, jnp.int32(1), jnp.int32(0))
    )

    def o_copy(i):
        return pltpu.make_async_remote_copy(
            src_ref=o.at[peer_of(i)],
            dst_ref=att.at[h],
            send_sem=o_ssem.at[i],
            recv_sem=o_rsem.at[h],
            device_id=(s, peer_of(i)),
            device_id_type=MESH,
        )

    own_o = pltpu.make_async_copy(o.at[h], att.at[h], own_sem)
    for i in list(range(2, H)) + [1]:
        o_copy(i).start()
    own_o.start()

    spots = lax.broadcasted_iota(jnp.int32, (T, T + 2 * FACE), 1).astype(F32)
    tap_lane = lax.broadcasted_iota(jnp.int32, (T, TAPS), 1)

    def build(t, _):
        want = jnp.sum(jnp.where(tap_lane == t, table[...].astype(F32), 0.0), axis=1, keepdims=True)
        onehot[t] = jnp.where(spots == want, F32(1.0), F32(0.0)).astype(BF16)
        return 0

    lax.fori_loop(0, TAPS, build, 0)

    def add_out(value, owner, first):
        part = jnp.dot(
            value, w_out[pl.ds(pl.multiple_of(owner * W, W), W), :], preferred_element_type=F32
        )
        acc[...] = part if first else acc[...] + part

    own_o.wait()
    add_out(att[h], h, True)
    for i in range(1, H):
        owner = peer_of(i)
        pltpu.make_async_copy(att.at[owner], att.at[owner], o_rsem.at[owner]).wait()
        add_out(att[owner], owner, False)

    own_live = active[s * H + h] * BLK

    def finish(r, _):
        rows = pl.ds(pl.multiple_of(r * RT, RT), RT)
        live = lax.broadcasted_iota(jnp.int32, (RT, 1), 0) + r * RT < own_live
        residual = tokens[rows, :].astype(F32) + attn_gate[...] * acc[rows, :]
        block_out[rows, :] = jnp.where(live, residual, 0.0).astype(BF16)
        return 0

    lax.fori_loop(0, T // RT, finish, 0)
    features = jnp.dot(block_out[...], w_dec[...], preferred_element_type=F32).astype(BF16)
    buf[0:T, :] = features

    slots = lax.broadcasted_iota(jnp.int32, (FACE, T), 1)
    for n, ref in enumerate((to_next, to_prev)):
        chosen = jnp.where(slots == ref[...], F32(1.0), F32(0.0)).astype(BF16)
        face[n] = jnp.dot(chosen, features, preferred_element_type=F32).astype(BF16)

    def face_copy(n, target):
        return pltpu.make_async_remote_copy(
            src_ref=face.at[n],
            dst_ref=buf.at[pl.ds(T + n * FACE, FACE), :],
            send_sem=face_ssem.at[n],
            recv_sem=face_rsem.at[n],
            device_id=target,
            device_id_type=MESH,
        )

    any_next = jnp.logical_or(has_next, h < H - 1)
    any_prev = jnp.logical_or(has_prev, h > 0)
    device = s * H + h

    @pl.when(any_next)
    def _():
        face_copy(0, ((device + 1) // H, (device + 1) % H)).start()

    @pl.when(any_prev)
    def _():
        face_copy(1, ((device - 1) // H, (device - 1) % H)).start()

    def face_arrival(n):
        rows = buf.at[pl.ds(T + n * FACE, FACE), :]
        pltpu.make_async_copy(rows, rows, face_rsem.at[n]).wait()

    for n, cond in ((0, any_prev), (1, any_next)):
        @pl.when(cond)
        def _():
            face_arrival(n)

        @pl.when(jnp.logical_not(cond))
        def _():
            buf[T + n * FACE : T + (n + 1) * FACE, :] = jnp.zeros((FACE, C), BF16)

    def tap(t, total):
        rows = jnp.dot(onehot[t], buf[...], preferred_element_type=F32).astype(BF16)
        return total + jnp.dot(rows, conv_w[t], preferred_element_type=F32)

    total = lax.fori_loop(0, TAPS, tap, buf[0:T, :].astype(F32))
    live = lax.broadcasted_iota(jnp.int32, (T, 1), 0) < own_live
    decoded[...] = jnp.where(live, total, 0.0).astype(BF16)

    for i in range(1, H):
        o_copy(i).wait_send()

    @pl.when(any_next)
    def _():
        face_copy(0, ((device + 1) // H, (device + 1) % H)).wait_send()

    @pl.when(any_prev)
    def _():
        face_copy(1, ((device - 1) // H, (device - 1) % H)).wait_send()


def body(
    tokens, mod_shift, mod_scale, attn_gate, w_qkv, query_gain, key_gain, w_out, w_dec,
    conv_weight, block_lists, active_blocks, to_next, to_prev, conv_table,
):
    S, H = lax.axis_size("seq"), lax.axis_size("head")
    T, D = tokens.shape
    W = D // H
    C = w_dec.shape[1]
    taps = conv_table.shape[1]
    face = to_next.shape[0]
    vmem = pl.BlockSpec(memory_space=pltpu.VMEM)
    smem = pl.BlockSpec(memory_space=pltpu.SMEM)
    hbm = pl.BlockSpec(memory_space=pl.ANY)
    dma = pltpu.SemaphoreType.DMA
    grant = 60 * 1024 * 1024
    q, kv = pl.pallas_call(
        functools.partial(project_kernel, S, H),
        out_shape=(
            jax.ShapeDtypeStruct((H, T, W), BF16),
            jax.ShapeDtypeStruct((2 * H, T, 2 * W), BF16),
        ),
        in_specs=[vmem] * 6,
        out_specs=(hbm, hbm),
        scratch_shapes=[
            pltpu.VMEM((T, D), BF16),
            pltpu.VMEM((H, T, 2 * W), BF16),
            pltpu.VMEM((H, T, W), BF16),
            dma((2,)),
            dma((H,)), dma((2 * H,)), dma((H,)),
            dma((H,)), dma((H,)),
        ],
        compiler_params=pltpu.CompilerParams(
            collective_id=0, has_side_effects=True, vmem_limit_bytes=grant
        ),
    )(
        tokens, mod_shift.reshape(1, D), mod_scale.reshape(1, D), w_qkv,
        query_gain.reshape(1, D), key_gain.reshape(1, D),
    )
    o = pl.pallas_call(
        attend_kernel,
        out_shape=jax.ShapeDtypeStruct((H, T, W), BF16),
        in_specs=[smem, smem, vmem, vmem],
        out_specs=vmem,
        compiler_params=pltpu.CompilerParams(vmem_limit_bytes=grant),
    )(block_lists, active_blocks, q, kv.reshape(2 * H * NB, BLK, 2 * W))
    return pl.pallas_call(
        functools.partial(finish_kernel, S, H),
        out_shape=(
            jax.ShapeDtypeStruct((T, D), BF16),
            jax.ShapeDtypeStruct((T, C), BF16),
        ),
        in_specs=[vmem, vmem, hbm, vmem, vmem, vmem, smem, vmem, vmem, vmem],
        out_specs=(vmem, vmem),
        scratch_shapes=[
            pltpu.VMEM((H, T, W), BF16),
            pltpu.VMEM((T, D), F32),
            pltpu.VMEM((taps, T, T + 2 * face), BF16),
            pltpu.VMEM((T + 2 * face, C), BF16),
            pltpu.VMEM((2, face, C), BF16),
            dma, dma((H,)), dma((H,)), dma((2,)), dma((2,)),
        ],
        compiler_params=pltpu.CompilerParams(
            collective_id=1, has_side_effects=True, vmem_limit_bytes=grant
        ),
    )(
        tokens, attn_gate.reshape(1, D), o, w_out, w_dec, conv_weight.reshape(taps, C, C),
        active_blocks, to_next.reshape(face, 1), to_prev.reshape(face, 1), conv_table,
    )


def solution(mesh):
    rows = P(("seq", "head"), None)
    return jax.shard_map(
        body,
        mesh=mesh,
        in_specs=(
            rows, P(), P(), P(), P(), P(), P(), P(), P(), P(),
            P("seq", None), P(), P(("seq", "head")), P(("seq", "head")), rows,
        ),
        out_specs=(rows, rows),
        check_vma=False,
    )
```

time: 439 us -> 117 us (0.27)
  local copies, waits for them, and re-layouts: 180 us -> 6.84 us
  Pallas kernels: 0 us -> 109 us
  waiting for transfers between devices: 97 us -> 0 us
  matrix products: 55.9 us -> 0 us
  other arithmetic: 51.4 us -> 0 us
  starting transfers between devices: 30.8 us -> 0 us
  blocking collectives: 17.9 us -> 0 us
    pallas_call x0 -> x3, Pallas kernels: none -> 109 us  [the longest x1 51.5 us: body(): pl.pallas_call(functools.partial(project_kernel, S, H), out_shape=(jax.Sh...]
    reshape x15 -> x2, local copies, waits for them, and re-layouts: 68.4 us -> 1.47 us  [the longest x1 0.74 us: body(): to_next.reshape(face, 1)]
    ppermute x4 -> x0, waiting for transfers between devices: 66 us -> none  [passed_along(): lax.ppermute(value, axis, [(source, source + steps) for source in range(l...]
    dot_general x12 -> x0, matrix products: 55.9 us -> none  [the longest x4 23.3 us: attend(): jnp.einsum('bqhd,bkhd->bhqk', queries, key_rows, preferred_element_type=j...]
    gather x7 -> x0, local copies, waits for them, and re-layouts: 52.3 us -> none  [the longest x1 28.4 us: body(): buffer[conv_table.reshape(-1)].reshape(slot_count, TAPS * channels)]
    all_to_all x3 -> x0, waiting for transfers between devices: 31.1 us -> none  [the longest x1 12.3 us: body(): lax.all_to_all(attended, 'head', split_axis=0, concat_axis=1, tiled=True)]
    sub x5 -> x0, other arithmetic: 26.5 us -> none  [the longest x4 26.5 us: attend(): raised = jnp.exp(scores - highest)]
    slice x5 -> x0, local copies, waits for them, and re-layouts: 20.8 us -> none  [the longest x4 19 us: one_step(): picked[:, :, local_width:].reshape(per_step, KB * BLK, heads_here, HD)]
  transfers between devices with their start and end apart: 7 -> 0, of which waited for: 5 -> 0; matrix products, arithmetic and copies ran while one was open for 3% -> 0% of each run, Pallas kernels for 0% -> 0%
where the time goes in v1:
time: 117 us; the launch traced here: 116 us
  Pallas kernels  109 us (93%)
  local copies, waits for them, and re-layouts  6.84 us (6%)
    pallas_call x1, Pallas kernels, body(): pl.pallas_call(functools.partial(project_kernel, S, H), out_shape=(jax.Sh...  51.5 us
    pallas_call x1, Pallas kernels, body(): pl.pallas_call(functools.partial(finish_kernel, S, H), out_shape=(jax.Sha...  42.2 us
    pallas_call x1, Pallas kernels, body(): pl.pallas_call(attend_kernel, out_shape=jax.ShapeDtypeStruct((H, T, W), B...  14.9 us
    unnamed x12, local copies, waits for them, and re-layouts  5.37 us

profile of v1, /device:TPU:3, one launch (start us, length us, event | category | flops | bytes accessed | tf_op | source)
XLA Modules:
  0.0 116.2 jit_solution(16625725772145423466)
XLA Ops:
  0.6 0.0 copy-start.1
  0.6 51.5 %shard_map.158 = (bf16[4,512,256]{2,1,0:T(8,128)(2,1)}, bf16[8,512,512]{2,1,0:T(8,128)(2,1)}) custom-call(bf16[512,1024]{1,0:T(8,128)(2,1)} %tokens.3, f32[1,1024]{1,0:T(1,128)} %bitcast.11, f32[1,1024]{1,0:T(1,128)} %bitcast.12, bf16[1024,3072]{1,0:T(8,128)(2,1)} %w_qkv.1, f32[1,1024]{1,0:T(1,128)} %bitcast.13, f32[1,1024]{1,0:T(1,128)} %bitcast.14), custom_call_target="tpu_custom_call" | custom-call | tf_op jit(solution)/shard_map/pallas_call | solution.py:402
  52.2 0.0 copy-start
  52.2 0.0 copy-start.2
  52.2 0.0 copy-start.3
  52.2 0.0 copy-done.1
  52.2 0.7 copy.17.lists
  52.9 14.9 %shard_map.159.o = bf16[4,512,256]{2,1,0:T(8,128)(2,1)} custom-call(s32[32,8]{1,0:T(8,128)} %copy.17.lists, s32[32]{0:T(128)} %active.3, bf16[4,512,256]{2,1,0:T(8,128)(2,1)} %get-tuple-element.4.q, bf16[64,64,512]{2,1,0:T(8,128)(2,1)} %bitcast.9), custom_call_target="tpu_custom_call" | custom-call | tf_op jit(solution)/shard_map/pallas_call | solution.py:425
  67.8 0.0 copy-done
  67.8 0.8 copy.20.table
  68.6 0.0 copy-done.2
  68.6 0.7 copy.18.to_next
  69.4 0.0 copy-done.3
  69.4 0.7 copy.19.to_prev
  70.1 42.2 %shard_map.160 = (bf16[512,1024]{1,0:T(8,128)(2,1)}, bf16[512,128]{1,0:T(8,128)(2,1)}) custom-call(bf16[512,1024]{1,0:T(8,128)(2,1)} %tokens.3, f32[1,1024]{1,0:T(1,128)} %bitcast.15, bf16[4,512,256]{2,1,0:T(8,128)(2,1)} %shard_map.159.o, bf16[1024,1024]{1,0:T(8,128)(2,1)} %w_out.1, bf16[1024,128]{1,0:T(8,128)(2,1)} %w_dec.1, ...), custom_call_target="tpu_custom_call" | custom-call | tf_op jit(solution)/shard_map/pallas_call | solution.py:432
  112.4 2.3 %copy.23 = bf16[512,1024]{1,0:T(8,128)(2,1)} copy(bf16[512,1024]{1,0:T(8,128)(2,1)} %get-tuple-element.8) | data formatting | bytes 2097152
  114.6 1.6 %copy.24 = bf16[512,128]{1,0:T(8,128)(2,1)} copy(bf16[512,128]{1,0:T(8,128)(2,1)} %get-tuple-element.9) | data formatting | bytes 262144
Async XLA Ops:
  0.6 51.6 %copy-start.1 = (s32[32,8]{0,1:T(8,128)S(1)}, s32[32,8]{0,1:T(8,128)}, u32[]{:S(2)}) copy-start(s32[32,8]{0,1:T(8,128)} %param.25) | copy-start | bytes 3076
  52.2 15.6 %copy-start = (s32[512,27]{0,1:T(8,128)S(1)}, s32[512,27]{0,1:T(8,128)}, u32[]{:S(2)}) copy-start(s32[512,27]{0,1:T(8,128)} %param.29) | copy-start | bytes 165892
  52.2 16.5 %copy-start.2 = (s32[128]{0:T(128)S(1)}, s32[128]{0:T(128)}, u32[]{:S(2)}) copy-start(s32[128]{0:T(128)} %param.27) | copy-start | bytes 1540
  52.2 17.2 %copy-start.3 = (s32[128]{0:T(128)S(1)}, s32[128]{0:T(128)}, u32[]{:S(2)}) copy-start(s32[128]{0:T(128)} %param.28) | copy-start | bytes 1540

commit v2 on v1

v2 whole, which is shorter than its diff:
```python
import functools
import math

import jax
import jax.numpy as jnp
from jax import lax
from jax.experimental import pallas as pl
from jax.experimental.pallas import tpu as pltpu
from jax.sharding import PartitionSpec as P

HD = 64
BLK = 64
NB = 8
KB = 8
EPSILON = 1e-06
MASKED = -1000000000.0
MESH = pl.DeviceIdType.MESH
BF16 = jnp.bfloat16
F32 = jnp.float32


class Group:
    def __init__(self, P, H):
        self.s, self.h = lax.axis_index("seq"), lax.axis_index("head")
        self.P, self.H, self.G, self.half = P, H, P * H, H // 2
        self.chips = self.G // 2
        self.first = self.s - self.s % P
        self.me = (self.s % P) * H + self.h
        self.chip, self.core = self.me // 2, self.me % 2
        self.others = [(0, 1)] + [(i, k) for i in range(1, self.chips) for k in range(2)]

    def chip_at(self, i):
        return (self.chip + i) % self.chips

    def core_at(self, k):
        return (self.core + k) % 2

    def member(self, i, k):
        return self.chip_at(i) * 2 + self.core_at(k)

    def place(self, i, k):
        member = self.member(i, k)
        return (self.first + member // self.H, member % self.H)


def ranges_per_group(S, H, D):
    return 2 if S % 2 == 0 and D // (2 * H) % 128 == 0 else 1


def project_kernel(
    S, H, P,
    tokens, mod_shift, mod_scale, w_qkv, q_gain, k_gain, lists,
    q, kv, all_lists,
    normed, kv_send, q_send, own_sem, list_ssem, list_rsem,
    kv_ssem, kv_rsem, f_ssem, q_ssem, q_rsem,
):
    T, D = tokens.shape
    g = Group(P, H)
    s, h, G, half = g.s, g.h, g.G, g.half
    W = D // G
    WIDE = 2 * W
    has_next, has_prev = g.first + P < S, g.first > 0

    barrier = pltpu.get_barrier_semaphore()
    for i, k in g.others:
        pl.semaphore_signal(barrier, inc=1, device_id=g.place(i, k), device_id_type=MESH)
    for cond, where in ((has_next, (s + P, h)), (has_prev, (s - P, h))):
        @pl.when(cond)
        def _():
            pl.semaphore_signal(barrier, inc=1, device_id=where, device_id_type=MESH)

    RT = 64

    def norm_rows(r, _):
        rows = pl.ds(pl.multiple_of(r * RT, RT), RT)
        x = tokens[rows, :].astype(F32)
        centred = x - jnp.mean(x, axis=-1, keepdims=True)
        spread = jnp.mean(centred * centred, axis=-1, keepdims=True)
        y = centred * lax.rsqrt(spread + EPSILON) * (1.0 + mod_scale[...]) + mod_shift[...]
        normed[rows, :] = y.astype(BF16)
        return 0

    lax.fori_loop(0, T // RT, norm_rows, 0)

    pl.semaphore_wait(
        barrier, G - 1 + jnp.where(has_next, jnp.int32(1), jnp.int32(0)) + jnp.where(has_prev, jnp.int32(1), jnp.int32(0))
    )

    same = (
        lax.broadcasted_iota(jnp.int32, (WIDE, WIDE), 0) // HD
        == lax.broadcasted_iota(jnp.int32, (WIDE, WIDE), 1) // HD
    )
    averaging = jnp.where(same, F32(1.0 / HD), F32(0.0)).astype(BF16)

    def head_norm(x, gain):
        square = x * x
        high = square.astype(BF16)
        low = (square - high.astype(F32)).astype(BF16)
        mean = jnp.dot(high, averaging, preferred_element_type=F32) + jnp.dot(
            low, averaging, preferred_element_type=F32
        )
        return (x * lax.rsqrt(mean + EPSILON) * gain).astype(BF16)

    PT = min(256, T)

    def columns(part, i):
        return pl.ds(pl.multiple_of(part * D + g.chip_at(i) * WIDE, WIDE), WIDE)

    def make_kv(i):
        def step(r, _):
            rows = pl.ds(pl.multiple_of(r * PT, PT), PT)
            x = normed[rows, :]
            key = jnp.dot(x, w_qkv[:, columns(1, i)], preferred_element_type=F32)
            key = head_norm(key, k_gain[:, columns(0, i)])
            val = jnp.dot(x, w_qkv[:, columns(2, i)], preferred_element_type=F32).astype(BF16)
            for core in range(2):
                kv_send[2 * i + core, rows, 0:W] = key[:, core * W : (core + 1) * W]
                kv_send[2 * i + core, rows, W : 2 * W] = val[:, core * W : (core + 1) * W]
            return 0

        lax.fori_loop(0, T // PT, step, 0)

    def make_q(i):
        def step(r, _):
            rows = pl.ds(pl.multiple_of(r * PT, PT), PT)
            x = jnp.dot(normed[rows, :], w_qkv[:, columns(0, i)], preferred_element_type=F32)
            x = head_norm(x, q_gain[:, columns(0, i)])
            for core in range(2):
                q_send[2 * i + core, rows, :] = x[:, core * W : (core + 1) * W]
            return 0

        lax.fori_loop(0, T // PT, step, 0)

    def kv_copy(i, k):
        return pltpu.make_async_remote_copy(
            src_ref=kv_send.at[2 * i + g.core_at(k)],
            dst_ref=kv.at[half + g.me],
            send_sem=kv_ssem.at[2 * i + k],
            recv_sem=kv_rsem.at[half + g.me],
            device_id=g.place(i, k),
            device_id_type=MESH,
        )

    def q_copy(i, k):
        return pltpu.make_async_remote_copy(
            src_ref=q_send.at[2 * i + g.core_at(k)],
            dst_ref=q.at[g.me],
            send_sem=q_ssem.at[2 * i + k],
            recv_sem=q_rsem.at[g.me],
            device_id=g.place(i, k),
            device_id_type=MESH,
        )

    def list_copy(n):
        return pltpu.make_async_remote_copy(
            src_ref=lists,
            dst_ref=all_lists.at[s % P],
            send_sem=list_ssem.at[n],
            recv_sem=list_rsem.at[s % P],
            device_id=(g.first + (s + n) % P, h),
            device_id_type=MESH,
        )

    def forward_copy(i, k, slot, target):
        own = (i, k) == (0, 0)
        return pltpu.make_async_remote_copy(
            src_ref=kv_send.at[g.core] if own else kv.at[half + g.member(i, k)],
            dst_ref=kv.at[slot],
            send_sem=f_ssem.at[2 * i + k],
            recv_sem=kv_rsem.at[slot],
            device_id=(target, h),
            device_id_type=MESH,
        )

    def each_forward(i, k, act):
        owner = g.member(i, k)

        @pl.when(jnp.logical_and(owner >= G - half, has_next))
        def _():
            act(forward_copy(i, k, owner - (G - half), s + P))

        @pl.when(jnp.logical_and(owner < half, has_prev))
        def _():
            act(forward_copy(i, k, half + G + owner, s - P))

    def arrival(ref, slot, sem):
        pltpu.make_async_copy(ref.at[slot], ref.at[slot], sem.at[slot]).wait()

    own_kv = pltpu.make_async_copy(kv_send.at[g.core], kv.at[half + g.me], own_sem.at[0])
    own_q = pltpu.make_async_copy(q_send.at[g.core], q.at[g.me], own_sem.at[1])
    own_list = pltpu.make_async_copy(lists, all_lists.at[s % P], own_sem.at[2])
    own_list.start()
    for n in range(1, P):
        list_copy(n).start()
    for i in list(range(1, g.chips)) + [0]:
        make_kv(i)
        for k in range(2) if i else (1,):
            kv_copy(i, k).start()
    each_forward(0, 0, lambda c: c.start())
    own_kv.start()
    for i in list(range(1, g.chips)) + [0]:
        make_q(i)
        for k in range(2) if i else (1,):
            q_copy(i, k).start()
    own_q.start()
    for i, k in [(0, 1)] + g.others[:0:-1]:
        arrival(kv, half + g.member(i, k), kv_rsem)
        each_forward(i, k, lambda c: c.start())
    for i, k in g.others:
        arrival(q, g.member(i, k), q_rsem)
    for n in range(1, P):
        arrival(all_lists, (s + n) % P, list_rsem)
    for j in range(half):
        @pl.when(has_prev)
        def _():
            arrival(kv, j, kv_rsem)

        @pl.when(has_next)
        def _():
            arrival(kv, half + G + j, kv_rsem)

    own_kv.wait()
    own_q.wait()
    own_list.wait()
    for n in range(1, P):
        list_copy(n).wait_send()
    for i, k in g.others:
        kv_copy(i, k).wait_send()
        q_copy(i, k).wait_send()
    for i, k in [(0, 0)] + g.others:
        each_forward(i, k, lambda c: c.wait_send())


def attend_kernel(half, P, lists, active, q, kv, o):
    G, T, W = q.shape
    heads = W // HD
    group = (lax.axis_index("seq") // P) * G
    o[...] = jnp.zeros_like(o)
    rows_of = lax.broadcasted_iota(jnp.int32, (heads * BLK, W), 0) // BLK
    lanes_of = lax.broadcasted_iota(jnp.int32, (heads * BLK, W), 1) // HD
    diagonal = jnp.where(rows_of == lanes_of, F32(1.0 / math.sqrt(HD)), F32(0.0)).astype(BF16)
    block_of = lax.broadcasted_iota(jnp.int32, (1, KB * BLK), 1) // BLK
    lane_head = lax.broadcasted_iota(jnp.int32, (BLK, W), 1) // HD
    base = (group - half) * NB

    def attend(owner, b):
        rows = pl.ds(pl.multiple_of(b * BLK, BLK), BLK)
        query = q[owner, rows, :]
        spread = jnp.concatenate([query] * heads, axis=0) * diagonal
        keys, values = [], []
        penalty = jnp.zeros((1, KB * BLK), F32)
        for n in range(KB):
            block = lists[owner * NB + b, n]
            live = lax.rem(block, NB) < active[block // NB]
            penalty = jnp.where(
                block_of == n, jnp.where(live, F32(0.0), F32(MASKED)), penalty
            )
            local = block - base
            keys.append(kv[local, :, 0:W])
            values.append(kv[local, :, W : 2 * W])
        scores = lax.dot_general(
            spread, jnp.concatenate(keys, axis=0), (((1,), (1,)), ((), ())),
            preferred_element_type=F32,
        ) + penalty
        raised = jnp.exp(scores - jnp.max(scores, axis=-1, keepdims=True))
        weights = (raised * (1.0 / jnp.sum(raised, axis=-1, keepdims=True))).astype(BF16)
        mixed = jnp.dot(weights, jnp.concatenate(values, axis=0), preferred_element_type=F32)
        result = mixed[0:BLK, :]
        for n in range(1, heads):
            result = jnp.where(lane_head == n, mixed[n * BLK : (n + 1) * BLK, :], result)
        o[owner, rows, :] = result.astype(BF16)

    def each_owner(owner, _):
        def pair(b, _):
            attend(owner, 2 * b)
            attend(owner, 2 * b + 1)
            return 0

        return lax.fori_loop(0, (active[group + owner] + 1) // 2, pair, 0)

    lax.fori_loop(0, G, each_owner, 0)


def finish_kernel(
    S, H, P,
    tokens, attn_gate, o, w_out, w_dec, conv_w, active, to_next, to_prev, table,
    block_out, decoded,
    att, acc, onehot, buf, face, own_sem, o_ssem, o_rsem, face_ssem, face_rsem,
):
    T, D = tokens.shape
    C = w_dec.shape[1]
    TAPS = table.shape[1]
    FACE = to_next.shape[1]
    RT = 64
    g = Group(P, H)
    s, h, G = g.s, g.h, g.G
    W = D // G
    has_next, has_prev = s < S - 1, s > 0
    wrap_next = jnp.logical_and(g.me == G - 1, has_next)
    wrap_prev = jnp.logical_and(g.me == 0, has_prev)

    barrier = pltpu.get_barrier_semaphore()
    for i, k in g.others:
        pl.semaphore_signal(barrier, inc=1, device_id=g.place(i, k), device_id_type=MESH)
    for cond, where in ((wrap_next, (s + 1, 0)), (wrap_prev, (s - 1, H - 1))):
        @pl.when(cond)
        def _():
            pl.semaphore_signal(barrier, inc=1, device_id=where, device_id_type=MESH)
    pl.semaphore_wait(
        barrier, G - 1 + jnp.where(wrap_next, jnp.int32(1), jnp.int32(0)) + jnp.where(wrap_prev, jnp.int32(1), jnp.int32(0))
    )

    def o_copy(i, k):
        return pltpu.make_async_remote_copy(
            src_ref=o.at[g.member(i, k)],
            dst_ref=att.at[g.me],
            send_sem=o_ssem.at[2 * i + k],
            recv_sem=o_rsem.at[g.me],
            device_id=g.place(i, k),
            device_id_type=MESH,
        )

    own_o = pltpu.make_async_copy(o.at[g.me], att.at[g.me], own_sem)
    for i, k in g.others[::-1]:
        o_copy(i, k).start()
    own_o.start()

    spots = lax.broadcasted_iota(jnp.int32, (T, T + 2 * FACE), 1).astype(F32)
    tap_lane = lax.broadcasted_iota(jnp.int32, (T, TAPS), 1)

    def build(t, _):
        want = jnp.sum(jnp.where(tap_lane == t, table[...].astype(F32), 0.0), axis=1, keepdims=True)
        onehot[t] = jnp.where(spots == want, F32(1.0), F32(0.0)).astype(BF16)
        return 0

    lax.fori_loop(0, TAPS, build, 0)

    own_o.wait()
    for i, k in g.others:
        owner = g.member(i, k)
        pltpu.make_async_copy(att.at[owner], att.at[owner], o_rsem.at[owner]).wait()
    attended = jnp.concatenate([att[n] for n in range(G)], axis=1)
    acc[...] = jnp.dot(attended, w_out[...], preferred_element_type=F32)

    own_live = active[s * H + h] * BLK

    def finish(r, _):
        rows = pl.ds(pl.multiple_of(r * RT, RT), RT)
        live = lax.broadcasted_iota(jnp.int32, (RT, 1), 0) + r * RT < own_live
        residual = tokens[rows, :].astype(F32) + attn_gate[...] * acc[rows, :]
        block_out[rows, :] = jnp.where(live, residual, 0.0).astype(BF16)
        return 0

    lax.fori_loop(0, T // RT, finish, 0)
    features = jnp.dot(block_out[...], w_dec[...], preferred_element_type=F32).astype(BF16)
    buf[0:T, :] = features

    slots = lax.broadcasted_iota(jnp.int32, (T, FACE), 0)
    for n, ref in enumerate((to_next, to_prev)):
        chosen = jnp.where(slots == ref[...], F32(1.0), F32(0.0)).astype(BF16)
        face[n] = lax.dot_general(
            chosen, features, (((0,), (0,)), ((), ())), preferred_element_type=F32
        ).astype(BF16)

    def face_copy(n, target):
        return pltpu.make_async_remote_copy(
            src_ref=face.at[n],
            dst_ref=buf.at[pl.ds(T + n * FACE, FACE), :],
            send_sem=face_ssem.at[n],
            recv_sem=face_rsem.at[n],
            device_id=target,
            device_id_type=MESH,
        )

    any_next = jnp.logical_or(has_next, h < H - 1)
    any_prev = jnp.logical_or(has_prev, h > 0)
    device = s * H + h

    @pl.when(any_next)
    def _():
        face_copy(0, ((device + 1) // H, (device + 1) % H)).start()

    @pl.when(any_prev)
    def _():
        face_copy(1, ((device - 1) // H, (device - 1) % H)).start()

    def face_arrival(n):
        rows = buf.at[pl.ds(T + n * FACE, FACE), :]
        pltpu.make_async_copy(rows, rows, face_rsem.at[n]).wait()

    for n, cond in ((0, any_prev), (1, any_next)):
        @pl.when(cond)
        def _():
            face_arrival(n)

        @pl.when(jnp.logical_not(cond))
        def _():
            buf[T + n * FACE : T + (n + 1) * FACE, :] = jnp.zeros((FACE, C), BF16)

    def tap(t, total):
        rows = jnp.dot(onehot[t], buf[...], preferred_element_type=F32).astype(BF16)
        return total + jnp.dot(rows, conv_w[t], preferred_element_type=F32)

    total = lax.fori_loop(0, TAPS, tap, buf[0:T, :].astype(F32))
    live = lax.broadcasted_iota(jnp.int32, (T, 1), 0) < own_live
    decoded[...] = jnp.where(live, total, 0.0).astype(BF16)

    for i, k in g.others:
        o_copy(i, k).wait_send()

    @pl.when(any_next)
    def _():
        face_copy(0, ((device + 1) // H, (device + 1) % H)).wait_send()

    @pl.when(any_prev)
    def _():
        face_copy(1, ((device - 1) // H, (device - 1) % H)).wait_send()


def body(
    tokens, mod_shift, mod_scale, attn_gate, w_qkv, query_gain, key_gain, w_out, w_dec,
    conv_weight, block_lists, active_blocks, to_next, to_prev, conv_table,
):
    S, H = lax.axis_size("seq"), lax.axis_size("head")
    T, D = tokens.shape
    P = ranges_per_group(S, H, D)
    G = P * H
    W = D // G
    GB = block_lists.shape[0]
    C = w_dec.shape[1]
    taps = conv_table.shape[1]
    face = to_next.shape[0]
    vmem = pl.BlockSpec(memory_space=pltpu.VMEM)
    smem = pl.BlockSpec(memory_space=pltpu.SMEM)
    hbm = pl.BlockSpec(memory_space=pl.ANY)
    dma = pltpu.SemaphoreType.DMA
    grant = 60 * 1024 * 1024
    q, kv, lists = pl.pallas_call(
        functools.partial(project_kernel, S, H, P),
        out_shape=(
            jax.ShapeDtypeStruct((G, T, W), BF16),
            jax.ShapeDtypeStruct((G + H, T, 2 * W), BF16),
            jax.ShapeDtypeStruct((P,) + block_lists.shape, jnp.int32),
        ),
        in_specs=[vmem] * 6 + [hbm],
        out_specs=(hbm, hbm, hbm),
        scratch_shapes=[
            pltpu.VMEM((T, D), BF16),
            pltpu.VMEM((G, T, 2 * W), BF16),
            pltpu.VMEM((G, T, W), BF16),
            dma((3,)), dma((P,)), dma((P,)),
            dma((G,)), dma((G + H,)), dma((G,)),
            dma((G,)), dma((G,)),
        ],
        compiler_params=pltpu.CompilerParams(
            collective_id=0, has_side_effects=True, vmem_limit_bytes=grant
        ),
    )(
        tokens, mod_shift.reshape(1, D), mod_scale.reshape(1, D), w_qkv,
        query_gain.reshape(1, D), key_gain.reshape(1, D), block_lists,
    )
    o = pl.pallas_call(
        functools.partial(attend_kernel, H // 2, P),
        out_shape=jax.ShapeDtypeStruct((G, T, W), BF16),
        in_specs=[smem, smem, vmem, vmem],
        out_specs=vmem,
        compiler_params=pltpu.CompilerParams(vmem_limit_bytes=grant),
    )(lists.reshape(P * GB, KB), active_blocks, q, kv.reshape((G + H) * NB, BLK, 2 * W))
    return pl.pallas_call(
        functools.partial(finish_kernel, S, H, P),
        out_shape=(
            jax.ShapeDtypeStruct((T, D), BF16),
            jax.ShapeDtypeStruct((T, C), BF16),
        ),
        in_specs=[vmem, vmem, hbm, vmem, vmem, vmem, smem, vmem, vmem, vmem],
        out_specs=(vmem, vmem),
        scratch_shapes=[
            pltpu.VMEM((G, T, W), BF16),
            pltpu.VMEM((T, D), F32),
            pltpu.VMEM((taps, T, T + 2 * face), BF16),
            pltpu.VMEM((T + 2 * face, C), BF16),
            pltpu.VMEM((2, face, C), BF16),
            dma, dma((G,)), dma((G,)), dma((2,)), dma((2,)),
        ],
        compiler_params=pltpu.CompilerParams(
            collective_id=1, has_side_effects=True, vmem_limit_bytes=grant
        ),
    )(
        tokens, attn_gate.reshape(1, D), o, w_out, w_dec, conv_weight.reshape(taps, C, C),
        active_blocks, to_next.reshape(1, face), to_prev.reshape(1, face), conv_table,
    )


def solution(mesh):
    rows = P(("seq", "head"), None)
    return jax.shard_map(
        body,
        mesh=mesh,
        in_specs=(
            rows, P(), P(), P(), P(), P(), P(), P(), P(), P(),
            P("seq", None), P(), P(("seq", "head")), P(("seq", "head")), rows,
        ),
        out_specs=(rows, rows),
        check_vma=False,
    )
```

time: 117 us -> 118 us (level)
  Pallas kernels: 109 us -> 111 us
    pallas_call x3, Pallas kernels: 109 us -> 111 us  [the longest x1 45.5 us: body(): pl.pallas_call(functools.partial(project_kernel, S, H, P), out_shape=(jax...]
    reshape x2 -> x0, local copies, waits for them, and re-layouts: 1.47 us -> none  [the longest x1 0.74 us: body(): to_next.reshape(face, 1)]
    unnamed x12 -> x6, local copies, waits for them, and re-layouts: 5.37 us -> 6.05 us
where the time goes in v2:
time: 118 us
  Pallas kernels  111 us (94%)
  local copies, waits for them, and re-layouts  6.05 us (5%)
    pallas_call x1, Pallas kernels, body(): pl.pallas_call(functools.partial(project_kernel, S, H, P), out_shape=(jax...  45.5 us
    pallas_call x1, Pallas kernels, body(): pl.pallas_call(functools.partial(finish_kernel, S, H, P), out_shape=(jax....  40.3 us
    pallas_call x1, Pallas kernels, body(): pl.pallas_call(functools.partial(attend_kernel, H // 2, P), out_shape=jax...  25.5 us
    unnamed x6, local copies, waits for them, and re-layouts  6.05 us

profile of v2, /device:TPU:3, one launch (start us, length us, event | category | flops | bytes accessed | tf_op | source)
XLA Modules:
  0.0 118.0 jit_solution(142118382907010005)
XLA Ops:
  0.6 1.4 %copy.17.lists = s32[32,8]{1,0:T(8,128)} copy(s32[32,8]{0,1:T(8,128)} %param.25) | data formatting | bytes 2048 | tf_op args[10]
  2.0 45.5 %shard_map.158 = (bf16[8,512,128]{2,1,0:T(8,128)(2,1)}, bf16[12,512,256]{2,1,0:T(8,128)(2,1)}, s32[2,32,8]{2,1,0:T(8,128)}) custom-call(bf16[512,1024]{1,0:T(8,128)(2,1)} %tokens.3, f32[1,1024]{1,0:T(1,128)} %bitcast.13, f32[1,1024]{1,0:T(1,128)} %bitcast.14, bf16[1024,3072]{1,0:T(8,128)(2,1)} %w_qkv.1, f32[1,1024]{1,0:T(1,128)} %bitcast.15, ...), custom_call_target="tpu_custom_call" | custom-call | tf_op jit(solution)/shard_map/pallas_call | solution.py:438
  47.5 0.0 copy-start
  47.6 25.5 %shard_map.159.o = bf16[8,512,128]{2,1,0:T(8,128)(2,1)} custom-call(s32[64,8]{1,0:T(8,128)} %bitcast.12, s32[32]{0:T(128)} %active.3, bf16[8,512,128]{2,1,0:T(8,128)(2,1)} %get-tuple-element.6.q, bf16[96,64,256]{2,1,0:T(8,128)(2,1)} %bitcast.10), custom_call_target="tpu_custom_call" | custom-call | tf_op jit(solution)/shard_map/pallas_call | solution.py:462
  73.0 0.0 copy-done
  73.0 0.9 copy.18.table
  73.9 40.3 %shard_map.160 = (bf16[512,1024]{1,0:T(8,128)(2,1)}, bf16[512,128]{1,0:T(8,128)(2,1)}) custom-call(bf16[512,1024]{1,0:T(8,128)(2,1)} %tokens.3, f32[1,1024]{1,0:T(1,128)} %bitcast.17, bf16[8,512,128]{2,1,0:T(8,128)(2,1)} %shard_map.159.o, bf16[1024,1024]{1,0:T(8,128)(2,1)} %w_out.1, bf16[1024,128]{1,0:T(8,128)(2,1)} %w_dec.1, ...), custom_call_target="tpu_custom_call" | custom-call | tf_op jit(solution)/shard_map/pallas_call | solution.py:469
  114.2 2.3 %copy.21 = bf16[512,1024]{1,0:T(8,128)(2,1)} copy(bf16[512,1024]{1,0:T(8,128)(2,1)} %get-tuple-element.10) | data formatting | bytes 2097152
  116.5 1.6 %copy.22 = bf16[512,128]{1,0:T(8,128)(2,1)} copy(bf16[512,128]{1,0:T(8,128)(2,1)} %get-tuple-element.11) | data formatting | bytes 262144
Async XLA Ops:
  47.5 25.5 %copy-start = (s32[512,27]{0,1:T(8,128)S(1)}, s32[512,27]{0,1:T(8,128)}, u32[]{:S(2)}) copy-start(s32[512,27]{0,1:T(8,128)} %param.29) | copy-start | bytes 165892

commit v3 on v2

--- a/solution.py
+++ b/solution.py
@@ -11,6 +11,8 @@
 HD = 64
 BLK = 64
 NB = 8
+STEP = 4
+UNROLL = 3
 KB = 8
 EPSILON = 1e-06
 MASKED = -1000000000.0
@@ -231,7 +233,7 @@
         each_forward(i, k, lambda c: c.wait_send())
 
 
-def attend_kernel(half, P, lists, active, q, kv, o):
+def attend_kernel(H, P, lists, active, q, kv, o):
     G, T, W = q.shape
     heads = W // HD
     group = (lax.axis_index("seq") // P) * G
@@ -241,42 +243,45 @@
     diagonal = jnp.where(rows_of == lanes_of, F32(1.0 / math.sqrt(HD)), F32(0.0)).astype(BF16)
     block_of = lax.broadcasted_iota(jnp.int32, (1, KB * BLK), 1) // BLK
     lane_head = lax.broadcasted_iota(jnp.int32, (BLK, W), 1) // HD
-    base = (group - half) * NB
-
-    def attend(owner, b):
-        rows = pl.ds(pl.multiple_of(b * BLK, BLK), BLK)
-        query = q[owner, rows, :]
-        spread = jnp.concatenate([query] * heads, axis=0) * diagonal
-        keys, values = [], []
-        penalty = jnp.zeros((1, KB * BLK), F32)
-        for n in range(KB):
-            block = lists[owner * NB + b, n]
-            live = lax.rem(block, NB) < active[block // NB]
-            penalty = jnp.where(
-                block_of == n, jnp.where(live, F32(0.0), F32(MASKED)), penalty
-            )
-            local = block - base
-            keys.append(kv[local, :, 0:W])
-            values.append(kv[local, :, W : 2 * W])
-        scores = lax.dot_general(
-            spread, jnp.concatenate(keys, axis=0), (((1,), (1,)), ((), ())),
-            preferred_element_type=F32,
-        ) + penalty
-        raised = jnp.exp(scores - jnp.max(scores, axis=-1, keepdims=True))
-        weights = (raised * (1.0 / jnp.sum(raised, axis=-1, keepdims=True))).astype(BF16)
-        mixed = jnp.dot(weights, jnp.concatenate(values, axis=0), preferred_element_type=F32)
-        result = mixed[0:BLK, :]
-        for n in range(1, heads):
-            result = jnp.where(lane_head == n, mixed[n * BLK : (n + 1) * BLK, :], result)
-        o[owner, rows, :] = result.astype(BF16)
+    base = (group - H // 2) * NB
+
+    def attend(owner, blocks):
+        queries, keys, values, penalties = [], [], [], []
+        for b in blocks:
+            rows = pl.ds(pl.multiple_of(b * BLK, BLK), BLK)
+            queries.append(jnp.concatenate([q[owner, rows, :]] * heads, axis=0) * diagonal)
+            picked, penalty = [], jnp.zeros((1, KB * BLK), F32)
+            for n in range(KB):
+                block = lists[owner // H, n, (owner % H) * NB + b]
+                live = lax.rem(block, NB) < active[block // NB]
+                penalty = jnp.where(
+                    block_of == n, jnp.where(live, F32(0.0), F32(MASKED)), penalty
+                )
+                picked.append(block - base)
+            keys.append(jnp.concatenate([kv[n, :, 0:W] for n in picked], axis=0))
+            values.append(jnp.concatenate([kv[n, :, W : 2 * W] for n in picked], axis=0))
+            penalties.append(penalty)
+        scores = [
+            lax.dot_general(x, y, (((1,), (1,)), ((), ())), preferred_element_type=F32) + z
+            for x, y, z in zip(queries, keys, penalties)
+        ]
+        raised = [jnp.exp(x - jnp.max(x, axis=-1, keepdims=True)) for x in scores]
+        weights = [
+            (x * (1.0 / jnp.sum(x, axis=-1, keepdims=True))).astype(BF16) for x in raised
+        ]
+        mixed = [jnp.dot(x, y, preferred_element_type=F32) for x, y in zip(weights, values)]
+        for b, x in zip(blocks, mixed):
+            result = x[0:BLK, :]
+            for n in range(1, heads):
+                result = jnp.where(lane_head == n, x[n * BLK : (n + 1) * BLK, :], result)
+            o[owner, pl.ds(pl.multiple_of(b * BLK, BLK), BLK), :] = result.astype(BF16)
 
     def each_owner(owner, _):
-        def pair(b, _):
-            attend(owner, 2 * b)
-            attend(owner, 2 * b + 1)
+        def step(b, _):
+            attend(owner, [STEP * b + n for n in range(STEP)])
             return 0
 
-        return lax.fori_loop(0, (active[group + owner] + 1) // 2, pair, 0)
+        return lax.fori_loop(0, (active[group + owner] + STEP - 1) // STEP, step, 0)
 
     lax.fori_loop(0, G, each_owner, 0)
 
@@ -329,11 +334,15 @@
     tap_lane = lax.broadcasted_iota(jnp.int32, (T, TAPS), 1)
 
     def build(t, _):
-        want = jnp.sum(jnp.where(tap_lane == t, table[...].astype(F32), 0.0), axis=1, keepdims=True)
-        onehot[t] = jnp.where(spots == want, F32(1.0), F32(0.0)).astype(BF16)
+        for n in range(UNROLL):
+            tap = t * UNROLL + n
+            want = jnp.sum(
+                jnp.where(tap_lane == tap, table[...].astype(F32), 0.0), axis=1, keepdims=True
+            )
+            onehot[tap] = jnp.where(spots == want, F32(1.0), F32(0.0)).astype(BF16)
         return 0
 
-    lax.fori_loop(0, TAPS, build, 0)
+    lax.fori_loop(0, TAPS // UNROLL, build, 0)
 
     own_o.wait()
     for i, k in g.others:
@@ -397,11 +406,22 @@
         def _():
             buf[T + n * FACE : T + (n + 1) * FACE, :] = jnp.zeros((FACE, C), BF16)
 
-    def tap(t, total):
-        rows = jnp.dot(onehot[t], buf[...], preferred_element_type=F32).astype(BF16)
-        return total + jnp.dot(rows, conv_w[t], preferred_element_type=F32)
-
-    total = lax.fori_loop(0, TAPS, tap, buf[0:T, :].astype(F32))
+    acc[:, 0:C] = buf[0:T, :].astype(F32)
+
+    def taps(t, _):
+        rows = jnp.concatenate(
+            [
+                jnp.dot(onehot[t * UNROLL + n], buf[...], preferred_element_type=F32).astype(BF16)
+                for n in range(UNROLL)
+            ],
+            axis=1,
+        )
+        weights = conv_w[pl.ds(pl.multiple_of(t * UNROLL * C, C), UNROLL * C), :]
+        acc[:, 0:C] += jnp.dot(rows, weights, preferred_element_type=F32)
+        return 0
+
+    lax.fori_loop(0, TAPS // UNROLL, taps, 0)
+    total = acc[:, 0:C]
     live = lax.broadcasted_iota(jnp.int32, (T, 1), 0) < own_live
     decoded[...] = jnp.where(live, total, 0.0).astype(BF16)
 
@@ -426,7 +446,6 @@
     P = ranges_per_group(S, H, D)
     G = P * H
     W = D // G
-    GB = block_lists.shape[0]
     C = w_dec.shape[1]
     taps = conv_table.shape[1]
     face = to_next.shape[0]
@@ -440,7 +459,7 @@
         out_shape=(
             jax.ShapeDtypeStruct((G, T, W), BF16),
             jax.ShapeDtypeStruct((G + H, T, 2 * W), BF16),
-            jax.ShapeDtypeStruct((P,) + block_lists.shape, jnp.int32),
+            jax.ShapeDtypeStruct((P, KB, block_lists.shape[0]), jnp.int32),
         ),
         in_specs=[vmem] * 6 + [hbm],
         out_specs=(hbm, hbm, hbm),
@@ -457,15 +476,15 @@
         ),
     )(
         tokens, mod_shift.reshape(1, D), mod_scale.reshape(1, D), w_qkv,
-        query_gain.reshape(1, D), key_gain.reshape(1, D), block_lists,
+        query_gain.reshape(1, D), key_gain.reshape(1, D), block_lists.T,
     )
     o = pl.pallas_call(
-        functools.partial(attend_kernel, H // 2, P),
+        functools.partial(attend_kernel, H, P),
         out_shape=jax.ShapeDtypeStruct((G, T, W), BF16),
         in_specs=[smem, smem, vmem, vmem],
         out_specs=vmem,
         compiler_params=pltpu.CompilerParams(vmem_limit_bytes=grant),
-    )(lists.reshape(P * GB, KB), active_blocks, q, kv.reshape((G + H) * NB, BLK, 2 * W))
+    )(lists, active_blocks, q, kv.reshape((G + H) * NB, BLK, 2 * W))
     return pl.pallas_call(
         functools.partial(finish_kernel, S, H, P),
         out_shape=(
@@ -486,7 +505,7 @@
             collective_id=1, has_side_effects=True, vmem_limit_bytes=grant
         ),
     )(
-        tokens, attn_gate.reshape(1, D), o, w_out, w_dec, conv_weight.reshape(taps, C, C),
+        tokens, attn_gate.reshape(1, D), o, w_out, w_dec, conv_weight,
         active_blocks, to_next.reshape(1, face), to_prev.reshape(1, face), conv_table,
     )
 

time: 118 us -> 102 us (0.86); the launches traced: 118 us -> 100 us
  Pallas kernels: 111 us -> 94.9 us
  local copies, waits for them, and re-layouts: 6.05 us -> 4.69 us
    pallas_call x1, Pallas kernels: 25.5 us -> 14.2 us  [body(): pl.pallas_call(functools.partial(attend_kernel, H, P), out_shape=jax.Shap...]
    pallas_call x1, Pallas kernels: 40.3 us -> 35.2 us  [body(): pl.pallas_call(functools.partial(finish_kernel, S, H, P), out_shape=(jax....]
    unnamed x6 -> x5, local copies, waits for them, and re-layouts: 6.05 us -> 4.69 us
where the time goes in v3:
time: 102 us; the launch traced here: 100 us
  Pallas kernels  94.9 us (93%)
  local copies, waits for them, and re-layouts  4.69 us (5%)
    pallas_call x1, Pallas kernels, body(): pl.pallas_call(functools.partial(project_kernel, S, H, P), out_shape=(jax...  45.5 us
    pallas_call x1, Pallas kernels, body(): pl.pallas_call(functools.partial(finish_kernel, S, H, P), out_shape=(jax....  35.2 us
    pallas_call x1, Pallas kernels, body(): pl.pallas_call(functools.partial(attend_kernel, H, P), out_shape=jax.Shap...  14.2 us
    unnamed x5, local copies, waits for them, and re-layouts  4.69 us

profile of v3, /device:TPU:3, one launch (start us, length us, event | category | flops | bytes accessed | tf_op | source)
XLA Modules:
  0.0 100.3 jit_solution(15750472978852050511)
XLA Ops:
  0.6 45.5 %shard_map.158 = (bf16[8,512,128]{2,1,0:T(8,128)(2,1)}, bf16[12,512,256]{2,1,0:T(8,128)(2,1)}, s32[2,8,32]{2,1,0:T(8,128)}) custom-call(bf16[512,1024]{1,0:T(8,128)(2,1)} %tokens.3, f32[1,1024]{1,0:T(1,128)} %bitcast.10, f32[1,1024]{1,0:T(1,128)} %bitcast.11, bf16[1024,3072]{1,0:T(8,128)(2,1)} %w_qkv.1, f32[1,1024]{1,0:T(1,128)} %bitcast.12, ...), custom_call_target="tpu_custom_call" | custom-call | tf_op jit(solution)/shard_map/pallas_call | solution.py:457
  46.2 0.0 copy-start
  46.2 14.2 %shard_map.159.o = bf16[8,512,128]{2,1,0:T(8,128)(2,1)} custom-call(s32[2,8,32]{2,1,0:T(8,128)} %get-tuple-element.5.lists, s32[32]{0:T(128)} %active.3, bf16[8,512,128]{2,1,0:T(8,128)(2,1)} %get-tuple-element.6.q, bf16[96,64,256]{2,1,0:T(8,128)(2,1)} %bitcast.9), custom_call_target="tpu_custom_call" | custom-call | tf_op jit(solution)/shard_map/pallas_call | solution.py:481
  60.4 0.0 copy-done
  60.4 0.9 copy.17.table
  61.2 35.2 %shard_map.160 = (bf16[512,1024]{1,0:T(8,128)(2,1)}, bf16[512,128]{1,0:T(8,128)(2,1)}) custom-call(bf16[512,1024]{1,0:T(8,128)(2,1)} %tokens.3, f32[1,1024]{1,0:T(1,128)} %bitcast.15, bf16[8,512,128]{2,1,0:T(8,128)(2,1)} %shard_map.159.o, bf16[1024,1024]{1,0:T(8,128)(2,1)} %w_out.1, bf16[1024,128]{1,0:T(8,128)(2,1)} %w_dec.1, bf16[3456,128]{1,0:T(8,128)(2,1)} %conv_w.1, ...), custom_call_target="tpu_custom_call" | custom-call | tf_op jit(solution)/shard_map/pallas_call | solution.py:488
  96.5 2.3 %copy.20 = bf16[512,1024]{1,0:T(8,128)(2,1)} copy(bf16[512,1024]{1,0:T(8,128)(2,1)} %get-tuple-element.10) | data formatting | bytes 2097152
  98.7 1.6 %copy.21 = bf16[512,128]{1,0:T(8,128)(2,1)} copy(bf16[512,128]{1,0:T(8,128)(2,1)} %get-tuple-element.11) | data formatting | bytes 262144
Async XLA Ops:
  46.2 14.2 %copy-start = (s32[512,27]{0,1:T(8,128)S(1)}, s32[512,27]{0,1:T(8,128)}, u32[]{:S(2)}) copy-start(s32[512,27]{0,1:T(8,128)} %param.29) | copy-start | bytes 165892
